TPU v7x, 1024 devices: a whole 8x8x8 slice. The times are simulated.
1024 devices in a mesh: seq: 128 (over y, x, core), head: 8 (over z).
Axes of the slice: x: 8, y: 8, z: 8, core: 2. Of those that a mesh axis runs over, the one named last changes fastest.
Arguments:
- queries: bfloat16 [1, 163840, 2048], P(None, ('seq', 'head')), may hold values from -6 to 6
- keys: bfloat16 [1, 163840, 2048], P(None, ('seq', 'head')), may hold values from -6 to 6
- values: bfloat16 [1, 163840, 2048], P(None, ('seq', 'head')), may hold values from -6 to 6
- decay_exp: int32 [16], replicated, may hold values from 0 to 11
- norm_gain: float32 [2048], P('head'), may hold values from 0.5 to 1.5
Outputs:
- attended: bfloat16 [1, 163840, 2048], P(None, 'seq', 'head')
All inputs are finite; a program needn't handle non-finite values.
Results may differ from a plain program's by a relative error of at most 0.0059.
Values may be sent and summed in bfloat16 or wider, within the bound.
A program may use at most 64 MiB of HBM per device.

v0:
```python
import jax
import jax.numpy as jnp
from jax import lax
from jax.sharding import PartitionSpec as P

HEADS = 16
DH = 128
BLOCK = 128


def prefix_2(part, axis, combine, identity):
    place = lax.axis_index(axis)
    gathered = jax.tree.map(lambda a: lax.all_gather(a, axis), part)
    state = jax.tree.map(lambda a, e: jnp.zeros_like(a) + jnp.asarray(e, a.dtype), part, identity)

    def one(hop, state):
        return combine(
            state, jax.tree.map(lambda a: lax.dynamic_index_in_dim(a, hop, 0, False), gathered)
        )

    return lax.fori_loop(0, place, one, state)


def key_terms(moved_keys, moved_values, rate):
    f32 = jnp.float32
    bf16 = jnp.bfloat16
    batch, length = (moved_keys.shape[0], moved_keys.shape[1])
    heads_here = rate.shape[0]
    nblk = length // BLOCK
    keys = moved_keys.reshape(batch, nblk, BLOCK, heads_here, DH)
    values = moved_values.reshape(batch, nblk, BLOCK, heads_here, DH)
    pos = jnp.arange(BLOCK).astype(f32)
    kfac = jnp.exp(-rate[None, :] * (BLOCK - 1 - pos)[:, None])
    kdec = (keys * kfac[:, :, None]).astype(bf16)
    pieces = jnp.einsum("bnjhd,bnjhe->bnhde", kdec, values, preferred_element_type=f32)
    index = jnp.arange(nblk).astype(f32)
    gap = index[:, None] - 1.0 - index[None, :]
    weights = jnp.where(
        gap >= 0, jnp.exp(-rate[:, None, None] * BLOCK * jnp.maximum(gap, 0.0)), 0.0
    )
    before = jnp.einsum("hmc,bchde->bmhde", weights, pieces, precision=lax.Precision.HIGHEST)
    tail = jnp.exp(-rate[:, None] * BLOCK * (nblk - 1.0 - index)[None, :])
    group_state = jnp.einsum("hc,bchde->bhde", tail, pieces, precision=lax.Precision.HIGHEST)
    return (keys, values, before, group_state)


def query_terms(moved_queries, keys, values, rate):
    f32 = jnp.float32
    bf16 = jnp.bfloat16
    batch, nblk = (keys.shape[0], keys.shape[1])
    heads_here = rate.shape[0]
    queries = moved_queries.reshape(batch, nblk, BLOCK, heads_here, DH)
    pos = jnp.arange(BLOCK).astype(f32)
    diff = pos[:, None] - pos[None, :]
    mask = jnp.where(diff >= 0, jnp.exp(-rate[:, None, None] * jnp.maximum(diff, 0.0)), 0.0)
    scores = jnp.einsum("bnihd,bnjhd->bnhij", queries, keys, preferred_element_type=f32)
    probs = (scores * mask).astype(bf16)
    intra = jnp.einsum("bnhij,bnjhd->bnihd", probs, values, preferred_element_type=f32)
    qfac = jnp.exp(-rate[None, :] * (pos + 1.0)[:, None])
    qdec = (queries * qfac[:, :, None]).astype(bf16)
    return (intra, qdec)


def finish(intra, before, qdec, incoming, rate, gain):
    f32 = jnp.float32
    batch, nblk = (intra.shape[0], intra.shape[1])
    index = jnp.arange(nblk).astype(f32)
    lift = jnp.exp(-rate[None, :] * BLOCK * index[:, None])
    prior = before + lift[None, :, :, None, None] * incoming[:, None]
    inter = jnp.einsum(
        "bnihd,bnhde->bnihe", qdec, prior.astype(jnp.bfloat16), preferred_element_type=f32
    )
    out = intra + inter
    scale = lax.rsqrt(jnp.mean(out * out, axis=-1, keepdims=True) + 1e-05)
    normed = out * scale * gain
    return normed.astype(jnp.bfloat16).reshape(batch, nblk * BLOCK, rate.shape[0] * DH)


def merge_power(earlier, later):
    return (earlier[0] * later[0], earlier[1] * later[0][None, :, None, None] + later[1])


def body(queries, keys, values, decay_exp, norm_gain):
    f32 = jnp.float32
    tok_here = queries.shape[1]
    n_seq = lax.axis_size("seq")
    n_head = lax.axis_size("head")
    total = tok_here * n_seq * n_head
    heads_here = HEADS // n_head
    first = lax.axis_index("head") * heads_here
    exps = lax.dynamic_slice_in_dim(decay_exp, first, heads_here)
    rate = jnp.exp2(exps.astype(f32)) / (2.0 * total)
    gain = norm_gain.reshape(heads_here, DH)
    length = tok_here * n_head
    power = jnp.exp(-rate * length)
    stacked = jnp.stack([queries, keys, values])
    moved = lax.all_to_all(stacked, "head", split_axis=3, concat_axis=2, tiled=True)
    moved_keys, moved_values = (moved[1], moved[2])
    local_keys, local_values, before, group_state = key_terms(moved_keys, moved_values, rate)
    ident = (jnp.ones_like(power), jnp.zeros_like(group_state))
    prefix = prefix_2((power, group_state), "seq", merge_power, ident)
    moved_queries = moved[0]
    intra, qdec = query_terms(moved_queries, local_keys, local_values, rate)
    return finish(intra, before, qdec, prefix[1], rate, gain)


def solution(mesh):
    return jax.shard_map(
        body,
        mesh=mesh,
        in_specs=(
            P(None, ("seq", "head"), None),
            P(None, ("seq", "head"), None),
            P(None, ("seq", "head"), None),
            P(),
            P("head"),
        ),
        out_specs=P(None, "seq", "head"),
        check_vma=False,
    )
```

profile of v0, /device:TPU:127, one launch (start us, length us, event | category | flops | bytes accessed | tf_op | source)
XLA Modules:
  0.0 503.6 jit_solution(17966494184059477537)
XLA Ops:
  6.5 1.7 pad_maximum_fusion
  8.2 4.7 copy.61
  12.9 8.4 %reshape.294 = bf16[8,2,61440]{2,1,0:T(2,128)(2,1)} reshape(bf16[2048,1,3,160]{3,2,1,0:T(4,128)(2,1)} %bitcast.52) | data formatting | bytes 3932160
  21.4 16.5 %all-to-all-start = ((bf16[8,2,61440]{2,1,0:T(2,128)(2,1)}), bf16[8,2,61440]{2,1,0:T(2,128)(2,1)S(1)}, u32[]{:S(2)}, u32[]{:S(2)}) async-start(bf16[8,2,61440]{2,1,0:T(2,128)(2,1)} %reshape.294), calls=%async_computation | async-start | bytes 3932160 | tf_op jit(solution)/shard_map/all_to_all | solution.py:97
  38.4 45.2 %all-to-all-done = bf16[8,2,61440]{2,1,0:T(2,128)(2,1)S(1)} async-done(((bf16[8,2,61440]{2,1,0:T(2,128)(2,1)}), bf16[8,2,61440]{2,1,0:T(2,128)(2,1)S(1)}, u32[]{:S(2)}, u32[]{:S(2)}) %all-to-all-start) | async-done | bytes 1966112 | tf_op jit(solution)/shard_map/all_to_all | solution.py:97
  83.6 6.5 %reshape.295 = bf16[2048,1,3,160]{3,2,1,0:T(4,128)(2,1)} reshape(bf16[8,2,61440]{2,1,0:T(2,128)(2,1)S(1)} %all-to-all-done) | data formatting | bytes 3932160
  90.1 4.9 copy.81
  97.6 3.0 fusion
  100.7 1.2 dynamic-slice
  102.6 247.4 %all-reduce = f32[256]{0:T(256)S(1)} all-reduce(f32[256]{0:T(256)S(1)} %exponential_dynamic-update-slice_fusion), channel_id=2, replica_groups=mesh['seq'=128,'head'=8] {'seq'}, use_global_device_ids=true, to_apply=%add | all-reduce | flops 256 | bytes 2048
  352.9 1.9 reshape.280
  354.8 1.5 multiply_convert_fusion.1
  356.3 2.1 fusion.12
  358.4 132.1 %while.12 = (s32[]{:T(128)}, f32[1,2,128,128]{3,2,1,0:T(8,128)S(1)}, s32[]{:T(128)}, f32[128,2]{1,0:T(8,128)S(1)}, f32[128,1,2,128,128]{4,3,2,1,0:T(8,128)}, /*index=5*/s32[]{:T(128)}, s32[]{:T(128)}, s32[]{:T(128)}) while((s32[]{:T(128)}, f32[1,2,128,128]{3,2,1,0:T(8,128)S(1)}, s32[]{:T(128)}, f32[128,2]{1,0:T(8,128)S(1)}, ...), condition=%wide.region_1.2_spmd, body=%wide.region_0.1_spmd.sunk | while | flops 65541 | bytes 393375 | solution.py:21
  361.6 1.0 bitcast_add_fusion.3
  362.6 1.0 bitcast_add_fusion.3
  363.7 1.0 bitcast_add_fusion.3
  364.7 1.0 bitcast_add_fusion.3
  365.8 1.0 bitcast_add_fusion.3
  366.8 1.0 bitcast_add_fusion.3
  367.8 1.0 bitcast_add_fusion.3
  368.9 1.0 bitcast_add_fusion.3
  369.9 1.0 bitcast_add_fusion.3
  371.0 1.0 bitcast_add_fusion.3
  372.0 1.0 bitcast_add_fusion.3
  373.0 1.0 bitcast_add_fusion.3
  374.1 1.0 bitcast_add_fusion.3
  375.1 1.0 bitcast_add_fusion.3
  376.1 1.0 bitcast_add_fusion.3
  381.3 1.0 bitcast_add_fusion.3
  382.4 1.0 bitcast_add_fusion.3
  383.4 1.0 bitcast_add_fusion.3
  384.5 1.0 bitcast_add_fusion.3
  385.5 1.0 bitcast_add_fusion.3
  386.5 1.0 bitcast_add_fusion.3
  387.6 1.0 bitcast_add_fusion.3
  388.6 1.0 bitcast_add_fusion.3
  389.6 1.0 bitcast_add_fusion.3
  390.7 1.0 bitcast_add_fusion.3
  391.7 1.0 bitcast_add_fusion.3
  392.8 1.0 bitcast_add_fusion.3
  393.8 1.0 bitcast_add_fusion.3
  394.8 1.0 bitcast_add_fusion.3
  395.9 1.0 bitcast_add_fusion.3
  401.1 1.0 bitcast_add_fusion.3
  402.1 1.0 bitcast_add_fusion.3
  490.6 3.0 fusion.8
  495.5 1.3 reshape.283
  (271 shorter events, 104.1 us)
Async XLA Ops:
  21.4 16.6 %copy-start.6 = (s32[16]{0:T(128)S(1)}, s32[16]{0:T(128)}, u32[]{:S(2)}) copy-start(s32[16]{0:T(128)} %param.10) | copy-start | bytes 196
  21.4 62.2 %all-to-all-start = ((bf16[8,2,61440]{2,1,0:T(2,128)(2,1)}), bf16[8,2,61440]{2,1,0:T(2,128)(2,1)S(1)}, u32[]{:S(2)}, u32[]{:S(2)}) async-start(bf16[8,2,61440]{2,1,0:T(2,128)(2,1)} %reshape.294), calls=%async_computation | async-start | bytes 3932160 | tf_op jit(solution)/shard_map/all_to_all | solution.py:97
  37.9 320.5 %all-gather.4.cloned.1.call-start = ((), (), s32[]{:S(2)}) async-start(), calls=%async_computation.1 | async-start | bytes 16908288 | tf_op jit(solution)/shard_map/all_gather | solution.py:13
  38.1 64.4 %copy-start.3 = (f32[2]{0:T(128)}, f32[2]{0:T(128)S(1)}, u32[]{:S(2)}) copy-start(f32[2]{0:T(128)S(1)} %get-tuple-element.81) | copy-start | bytes 28
  97.6 254.4 %copy-start.2 = (bf16[1,1,8,160,256]{4,2,3,0,1:T(8,128)(2,1)S(1)}, bf16[1,1,8,160,256]{4,2,3,0,1:T(8,128)(2,1)}, u32[]{:S(2)}) copy-start(bf16[1,1,8,160,256]{4,2,3,0,1:T(8,128)(2,1)} %get-tuple-element.84) | copy-start | bytes 1966084
  358.4 132.1 %copy-start.4 = (f32[10,2]{0,1:T(2,128)S(1)}, f32[10,2]{0,1:T(2,128)}, u32[]{:S(2)}) copy-start(f32[10,2]{0,1:T(2,128)} %multiply_exponential_fusion.2) | copy-start | bytes 244
  490.5 3.1 copy-start
  490.5 3.1 copy-start.1
  493.6 0.7 copy-start.5
Sparse Core Ops, SparseCore 0:
  100.7 102.4 all-gather.3
where the time goes:
time: 506 us; the launch traced here: 504 us
  blocking collectives  247 us (49%)
  other arithmetic  133 us (26%)
  waiting for transfers between devices  45.2 us (9%)
  local copies, waits for them, and re-layouts  34.3 us (7%)
  starting transfers between devices  16.6 us (3%)
  between operations  14.2 us (3%)
  matrix products  9.17 us (2%)
    unnamed x1, blocking collectives  247 us
    add x127, other arithmetic, merge_power(): earlier[1] * later[0][None, :, None, None] + later[1]  127 us
    all_to_all x1, waiting for transfers between devices, body(): lax.all_to_all(stacked, 'head', split_axis=3, concat_axis=2, tiled=True)  45.2 us
    all_to_all x1, starting transfers between devices, body(): lax.all_to_all(stacked, 'head', split_axis=3, concat_axis=2, tiled=True)  16.5 us
    unnamed x18, local copies, waits for them, and re-layouts  16.2 us
  transfers between devices with their start and end apart: 2, of which 1 were waited for; matrix products, arithmetic and copies ran while one was open for 2% of the time, Pallas kernels for 0%

commit v1 on v0

v1 whole, which is shorter than its diff:
```python
import functools

import jax
import jax.numpy as jnp
from jax import lax
from jax.experimental import pallas as pl
from jax.experimental.pallas import tpu as pltpu
from jax.sharding import PartitionSpec as P

HEADS = 16
DH = 128
BLOCK = 128
NX = 8
CORES = 2
MESH = pl.DeviceIdType.MESH
F32 = jnp.float32
BF16 = jnp.bfloat16


def power_of_two(e):
    r = jnp.float32(1.0)
    for bit in range(4):
        r = r * jnp.where((e >> bit) & 1 == 1, jnp.float32(2.0 ** (2**bit)), jnp.float32(1.0))
    return r


def nt(a, b):
    return lax.dot_general(a, b, (((1,), (1,)), ((), ())), preferred_element_type=F32)


def tn(a, b):
    return lax.dot_general(a, b, (((0,), (0,)), ((), ())), preferred_element_type=F32)


def nn(a, b):
    return jnp.dot(a, b, preferred_element_type=F32)


def kernel(
    n_z,
    n_y,
    total,
    q_hbm,
    k_hbm,
    v_hbm,
    dec_ref,
    gain_ref,
    out_ref,
    qb,
    kb,
    vb,
    before,
    intra,
    mask,
    kfac,
    qfac,
    gbuf,
    pair_in,
    xbuf,
    ybuf,
    last_out,
    last_in,
    local_sem,
    z_send,
    z_recv,
    x_send,
    x_recv,
    y_send,
    y_recv,
    p_send,
    p_recv,
):
    s = lax.axis_index("seq")
    z = lax.axis_index("head")
    core = lax.rem(s, CORES)
    x = lax.rem(lax.div(s, CORES), NX)
    y = lax.div(s, CORES * NX)
    part = q_hbm.shape[0]
    wide = q_hbm.shape[1] // n_z
    length = part * n_z
    nblk = length // BLOCK
    heads_here = wide // DH

    def seq_of(yy, xx, cc):
        return (yy * NX + xx) * CORES + cc

    def at_z(d):
        return (s, lax.rem(z + d, n_z))

    def at_x(d):
        return (seq_of(y, lax.rem(x + d, NX), core), z)

    def at_y(d):
        return (seq_of(lax.rem(y + d, n_y), x, core), z)

    partner = (seq_of(y, x, 1 - core), z)

    hbm = (k_hbm, v_hbm, q_hbm)
    vmem = (kb, vb, qb)
    own_cols = pl.ds(pl.multiple_of(z * wide, wide), wide)
    own_rows = pl.ds(pl.multiple_of(z * part, part), part)
    locals_ = []
    for a in range(3):
        copy = pltpu.make_async_copy(hbm[a].at[:, own_cols], vmem[a].at[own_rows], local_sem.at[a])
        copy.start()
        locals_.append(copy)

    barrier = pltpu.get_barrier_semaphore()
    for d in range(1, n_z):
        pl.semaphore_signal(barrier, inc=1, device_id=at_z(d), device_id_type=MESH)
    for d in range(1, NX):
        pl.semaphore_signal(barrier, inc=1, device_id=at_x(d), device_id_type=MESH)
    for d in range(1, n_y):
        pl.semaphore_signal(barrier, inc=1, device_id=at_y(d), device_id_type=MESH)
    pl.semaphore_signal(barrier, inc=1, device_id=partner, device_id_type=MESH)
    pl.semaphore_wait(barrier, n_z + NX + n_y - 2)

    order = sorted(range(1, n_z), key=lambda d: (-min(d, n_z - d), d))
    z_copies = []
    for a in range(3):
        copies = []
        for d in order:
            to = lax.rem(z + d, n_z)
            copy = pltpu.make_async_remote_copy(
                src_ref=hbm[a].at[:, pl.ds(pl.multiple_of(to * wide, wide), wide)],
                dst_ref=vmem[a].at[own_rows],
                send_sem=z_send.at[a, d],
                recv_sem=z_recv.at[a, d],
                device_id=(s, to),
                device_id_type=MESH,
            )
            copy.start()
            copies.append(copy)
        z_copies.append(copies)

    row = lax.broadcasted_iota(jnp.int32, (BLOCK, BLOCK), 0).astype(F32)
    col = lax.broadcasted_iota(jnp.int32, (BLOCK, BLOCK), 1).astype(F32)
    diff = row - col
    rates = []
    for h in range(heads_here):
        rate = power_of_two(dec_ref[z * heads_here + h]) / jnp.float32(2.0 * total)
        rates.append(rate)
        mask[h] = jnp.where(diff >= 0, jnp.exp(-rate * jnp.maximum(diff, 0.0)), 0.0)
        kfac[h] = jnp.exp(-rate * (BLOCK - 1 - row))
        qfac[h] = jnp.exp(-rate * (row + 1.0))
    rate_here = jnp.where(core == 0, rates[0], rates[1])

    def decay(rate, tokens):
        return jnp.exp(jnp.full((1, DH), -rate * tokens, F32))

    for a in (0, 1):
        locals_[a].wait()
        for copy in z_copies[a]:
            copy.wait_recv()

    step_decay = [decay(rates[h], BLOCK) for h in range(heads_here)]

    def state_step(b, states):
        rows = pl.ds(pl.multiple_of(b * BLOCK, BLOCK), BLOCK)
        fresh = []
        for h in range(heads_here):
            cols = slice(h * DH, (h + 1) * DH)
            before[h, b] = states[h]
            kdec = (kb[rows, cols].astype(F32) * kfac[h]).astype(BF16)
            fresh.append(states[h] * step_decay[h] + tn(kdec, vb[rows, cols]))
        return tuple(fresh)

    zero = jnp.zeros((DH, DH), F32)
    group = lax.fori_loop(0, nblk, state_step, (zero,) * heads_here)
    for h in range(heads_here):
        gbuf[h] = group[h]

    pair = pltpu.make_async_remote_copy(
        src_ref=gbuf.at[1 - core],
        dst_ref=pair_in,
        send_sem=p_send.at[0],
        recv_sem=p_recv.at[0],
        device_id=partner,
        device_id_type=MESH,
    )
    pair.start()
    w1 = decay(rate_here, length)
    pair.wait_recv()
    mine = gbuf[core]
    theirs = pair_in[...]
    first = jnp.where(core == 0, mine, theirs)
    second = jnp.where(core == 0, theirs, mine)
    xbuf[x] = (first * w1 + second).astype(BF16)
    x_copies = []
    for d in range(1, NX):
        copy = pltpu.make_async_remote_copy(
            src_ref=xbuf.at[x],
            dst_ref=xbuf.at[x],
            send_sem=x_send.at[d],
            recv_sem=x_recv.at[d],
            device_id=at_x(d),
            device_id_type=MESH,
        )
        copy.start()
        x_copies.append(copy)
    for copy in x_copies:
        copy.wait_recv()
    chip = CORES * length
    in_row = jnp.zeros((DH, DH), F32)
    row_total = jnp.zeros((DH, DH), F32)
    for i in range(NX):
        state = xbuf[i].astype(F32)
        gap = jnp.maximum(x - 1 - i, 0).astype(F32)
        in_row += state * jnp.where(i < x, decay(rate_here, chip * gap), 0.0)
        row_total += state * decay(rate_here, chip * (NX - 1.0 - i))
    ybuf[y] = row_total.astype(BF16)

    def y_copy(d):
        return pltpu.make_async_remote_copy(
            src_ref=ybuf.at[y],
            dst_ref=ybuf.at[y],
            send_sem=y_send.at[d],
            recv_sem=y_recv.at[d],
            device_id=at_y(d),
            device_id_type=MESH,
        )

    for d in range(1, n_y):
        y_copy(d).start()

    locals_[2].wait()
    for copy in z_copies[2]:
        copy.wait_recv()

    def intra_step(b, carry):
        rows = pl.ds(pl.multiple_of(b * BLOCK, BLOCK), BLOCK)
        for h in range(heads_here):
            cols = slice(h * DH, (h + 1) * DH)
            probs = (nt(qb[rows, cols], kb[rows, cols]) * mask[h]).astype(BF16)
            intra[rows, cols] = nn(probs, vb[rows, cols])
        return carry

    lax.fori_loop(0, nblk, intra_step, 0)

    for d in range(1, n_y):
        y_copy(d).wait_recv()
    above = jnp.zeros((DH, DH), F32)
    for i in range(n_y):
        gap = jnp.maximum(y - 1 - i, 0).astype(F32)
        above += ybuf[i].astype(F32) * jnp.where(i < y, decay(rate_here, chip * NX * gap), 0.0)
    incoming = above * decay(rate_here, chip * x.astype(F32)) + in_row
    after = incoming * w1 + first
    last_out[...] = jnp.where(core == 0, after, incoming)
    last = pltpu.make_async_remote_copy(
        src_ref=last_out,
        dst_ref=last_in,
        send_sem=p_send.at[1],
        recv_sem=p_recv.at[1],
        device_id=partner,
        device_id_type=MESH,
    )
    last.start()

    def finish(h, rate, state):
        cols = pl.ds(pl.multiple_of(h * DH, DH), DH)
        gain = gain_ref[:, cols]
        fac = qfac[h]

        def step(b, carry):
            rows = pl.ds(pl.multiple_of(b * BLOCK, BLOCK), BLOCK)
            lift = decay(rate, BLOCK * b.astype(F32))
            prior = (before[h, b] + lift * state).astype(BF16)
            qdec = (qb[rows, cols].astype(F32) * fac).astype(BF16)
            o = intra[rows, cols] + nn(qdec, prior)
            scale = lax.rsqrt(jnp.mean(o * o, axis=-1, keepdims=True) + 1e-05)
            out_ref[rows, cols] = (o * scale * gain).astype(BF16)
            return carry

        lax.fori_loop(0, nblk, step, 0)

    finish(core, rate_here, jnp.where(core == 0, incoming, after))
    last.wait_recv()
    finish(1 - core, jnp.where(core == 0, rates[1], rates[0]), last_in[...])

    for copies in z_copies:
        for copy in copies:
            copy.wait_send()
    for copy in x_copies:
        copy.wait_send()
    for d in range(1, n_y):
        y_copy(d).wait_send()
    pair.wait_send()
    last.wait_send()


def body(queries, keys, values, decay_exp, norm_gain):
    _, part, width = queries.shape
    n_z = lax.axis_size("head")
    n_seq = lax.axis_size("seq")
    n_y = n_seq // (NX * CORES)
    wide = width // n_z
    heads_here = wide // DH
    length = part * n_z
    nblk = length // BLOCK
    total = length * n_seq
    square = (DH, DH)
    out = pl.pallas_call(
        functools.partial(kernel, n_z, n_y, total),
        out_shape=jax.ShapeDtypeStruct((length, wide), BF16),
        in_specs=[pl.BlockSpec(memory_space=pltpu.HBM)] * 3
        + [pl.BlockSpec(memory_space=pltpu.SMEM), pl.BlockSpec(memory_space=pltpu.VMEM)],
        out_specs=pl.BlockSpec(memory_space=pltpu.VMEM),
        scratch_shapes=[
            pltpu.VMEM((length, wide), BF16),
            pltpu.VMEM((length, wide), BF16),
            pltpu.VMEM((length, wide), BF16),
            pltpu.VMEM((heads_here, nblk) + square, F32),
            pltpu.VMEM((length, wide), F32),
            pltpu.VMEM((heads_here,) + square, F32),
            pltpu.VMEM((heads_here,) + square, F32),
            pltpu.VMEM((heads_here,) + square, F32),
            pltpu.VMEM((heads_here,) + square, F32),
            pltpu.VMEM(square, F32),
            pltpu.VMEM((NX,) + square, BF16),
            pltpu.VMEM((n_y,) + square, BF16),
            pltpu.VMEM(square, F32),
            pltpu.VMEM(square, F32),
            pltpu.SemaphoreType.DMA((3,)),
            pltpu.SemaphoreType.DMA((3, n_z)),
            pltpu.SemaphoreType.DMA((3, n_z)),
            pltpu.SemaphoreType.DMA((NX,)),
            pltpu.SemaphoreType.DMA((NX,)),
            pltpu.SemaphoreType.DMA((n_y,)),
            pltpu.SemaphoreType.DMA((n_y,)),
            pltpu.SemaphoreType.DMA((2,)),
            pltpu.SemaphoreType.DMA((2,)),
        ],
        compiler_params=pltpu.CompilerParams(collective_id=0, has_side_effects=True),
    )(
        queries.reshape(part, width),
        keys.reshape(part, width),
        values.reshape(part, width),
        decay_exp,
        norm_gain.reshape(1, wide),
    )
    return out.reshape(1, length, wide)


def solution(mesh):
    return jax.shard_map(
        body,
        mesh=mesh,
        in_specs=(
            P(None, ("seq", "head"), None),
            P(None, ("seq", "head"), None),
            P(None, ("seq", "head"), None),
            P(),
            P("head"),
        ),
        out_specs=P(None, "seq", "head"),
        check_vma=False,
    )
```

time: 506 us -> 86.1 us (0.17)
  the two profiles are of different devices: /device:TPU:127 before, /device:TPU:1 now
where the time goes in v1:
time: 86.1 us; the launch traced here: 85.9 us
  Pallas kernels  84 us (98%)
  local copies, waits for them, and re-layouts  1.97 us (2%)
    pallas_call x1, Pallas kernels, body(): pl.pallas_call(functools.partial(kernel, n_z, n_y, total), out_shape=jax....  84 us
    unnamed x1, local copies, waits for them, and re-layouts  1.97 us

profile of v1, /device:TPU:1, one launch (start us, length us, event | category | flops | bytes accessed | tf_op | source)
XLA Modules:
  0.0 85.9 jit_solution(11704060720479457649)
XLA Ops:
  0.0 84.0 %shard_map.55 = bf16[1280,256]{1,0:T(8,128)(2,1)} custom-call(bf16[160,2048]{1,0:T(8,128)(2,1)} %bitcast.6, bf16[160,2048]{1,0:T(8,128)(2,1)} %bitcast.7, bf16[160,2048]{1,0:T(8,128)(2,1)} %bitcast.8, s32[16]{0:T(128)} %dec_ref.1, f32[1,256]{1,0:T(1,128)} %bitcast.9), custom_call_target="tpu_custom_call" | custom-call | tf_op jit(solution)/shard_map/pallas_call | solution.py:302
  84.0 2.0 %copy.7 = bf16[1,1280,256]{2,1,0:T(8,128)(2,1)} copy(bf16[1,1280,256]{2,1,0:T(8,128)(2,1)} %bitcast.5) | data formatting | bytes 1310720

commit v2 on v1

v2 whole, which is shorter than its diff:
```python
import functools

import jax
import jax.numpy as jnp
from jax import lax
from jax.experimental import pallas as pl
from jax.experimental.pallas import tpu as pltpu
from jax.sharding import PartitionSpec as P

HEADS = 16
DH = 128
NX = 8
CORES = 2
MESH = pl.DeviceIdType.MESH
F32 = jnp.float32
BF16 = jnp.bfloat16


def power_of_two(e):
    r = jnp.float32(1.0)
    for bit in range(4):
        r = r * jnp.where((e >> bit) & 1 == 1, jnp.float32(2.0 ** (2**bit)), jnp.float32(1.0))
    return r


def nt(a, b):
    return lax.dot_general(a, b, (((1,), (1,)), ((), ())), preferred_element_type=F32)


def tn(a, b):
    return lax.dot_general(a, b, (((0,), (0,)), ((), ())), preferred_element_type=F32)


def nn(a, b):
    return jnp.dot(a, b, preferred_element_type=F32)


def kernel(
    n_z,
    n_y,
    total,
    q_hbm,
    k_hbm,
    v_hbm,
    dec_ref,
    gain_ref,
    out_ref,
    qf,
    kf,
    vf,
    state_out,
    state_in,
    intra_out,
    intra_in,
    q_in,
    near,
    fall,
    gbuf,
    pair_in,
    xbuf,
    ybuf,
    last_out,
    last_in,
    local_sem,
    z_send,
    z_recv,
    x_send,
    x_recv,
    y_send,
    y_recv,
    p_send,
    p_recv,
):
    s = lax.axis_index("seq")
    z = lax.axis_index("head")
    core = lax.rem(s, CORES)
    x = lax.rem(lax.div(s, CORES), NX)
    y = lax.div(s, CORES * NX)
    part = q_hbm.shape[0]
    wide = q_hbm.shape[1] // n_z
    length = part * n_z
    heads_here = wide // DH

    def seq_of(yy, xx, cc):
        return (yy * NX + xx) * CORES + cc

    def at_z(d):
        return (s, lax.rem(z + d, n_z))

    def at_x(d):
        return (seq_of(y, lax.rem(x + d, NX), core), z)

    def at_y(d):
        return (seq_of(lax.rem(y + d, n_y), x, core), z)

    partner = (seq_of(y, x, 1 - core), z)

    own_cols = pl.ds(pl.multiple_of(z * wide, wide), wide)
    own_rows = pl.ds(pl.multiple_of(z * part, part), part)
    loads = []
    for a, (src, dst) in enumerate(
        ((k_hbm, kf), (v_hbm, vf), (q_hbm, qf), (q_hbm.at[:, own_cols], q_in.at[own_rows]))
    ):
        copy = pltpu.make_async_copy(src, dst, local_sem.at[a])
        copy.start()
        loads.append(copy)

    barrier = pltpu.get_barrier_semaphore()
    for d in range(1, n_z):
        pl.semaphore_signal(barrier, inc=1, device_id=at_z(d), device_id_type=MESH)
    for d in range(1, NX):
        pl.semaphore_signal(barrier, inc=1, device_id=at_x(d), device_id_type=MESH)
    for d in range(1, n_y):
        pl.semaphore_signal(barrier, inc=1, device_id=at_y(d), device_id_type=MESH)
    pl.semaphore_signal(barrier, inc=1, device_id=partner, device_id_type=MESH)

    order = sorted(range(1, n_z), key=lambda d: (-min(d, n_z - d), d))

    def rate_of(head):
        return power_of_two(dec_ref[head]) / jnp.float32(2.0 * total)

    def decay(rate, tokens):
        return jnp.exp(jnp.full((1, DH), -rate * tokens, F32))

    place = lax.broadcasted_iota(jnp.int32, (part, DH), 0).astype(F32)
    loads[0].wait()
    loads[1].wait()
    for d in order + [0]:
        to = lax.rem(z + d, n_z)
        for h in range(heads_here):
            head = to * heads_here + h
            cols = pl.ds(pl.multiple_of(head * DH, DH), DH)
            rate = rate_of(head)
            grown = vf[:, cols].astype(F32) * jnp.exp(rate * (place + 1.0))
            high = grown.astype(BF16)
            low = (grown - high.astype(F32)).astype(BF16)
            both = tn(kf[:, cols], jnp.concatenate([high, low], axis=1))
            state = (both[:, :DH] + both[:, DH:]) * decay(rate, part)
            state_out[to, h] = state.astype(BF16)

    pl.semaphore_wait(barrier, n_z + NX + n_y - 2)

    def z_copy(a, d):
        to = lax.rem(z + d, n_z)
        if a == 0:
            src, dst = state_out.at[to], state_in.at[z]
        elif a == 1:
            src, dst = q_hbm.at[:, pl.ds(pl.multiple_of(to * wide, wide), wide)], q_in.at[own_rows]
        else:
            src, dst = intra_out.at[to], intra_in.at[own_rows]
        return pltpu.make_async_remote_copy(
            src_ref=src,
            dst_ref=dst,
            send_sem=z_send.at[a, d],
            recv_sem=z_recv.at[a, d],
            device_id=(s, to),
            device_id_type=MESH,
        )

    for a in (0, 1):
        for d in order:
            z_copy(a, d).start()
    own_state = pltpu.make_async_copy(state_out.at[z], state_in.at[z], local_sem.at[4])
    own_state.start()

    loads[2].wait()
    row = lax.broadcasted_iota(jnp.int32, (part, part), 0)
    col = lax.broadcasted_iota(jnp.int32, (part, part), 1)
    causal = col <= row
    key_place = lax.broadcasted_iota(jnp.int32, (1, part), 1).astype(F32)
    for d in order + [0]:
        to = lax.rem(z + d, n_z)
        for h in range(heads_here):
            head = to * heads_here + h
            cols = pl.ds(pl.multiple_of(head * DH, DH), DH)
            rise = jnp.exp(rate_of(head) * (key_place + 1.0))
            scores = nt(qf[:, cols], kf[:, cols])
            probs = jnp.where(causal, scores * rise, 0.0).astype(BF16)
            intra_out[to, :, h * DH : (h + 1) * DH] = nn(probs, vf[:, cols]).astype(BF16)
        if d:
            z_copy(2, d).start()
    own_intra = pltpu.make_async_copy(intra_out.at[z], intra_in.at[own_rows], local_sem.at[5])
    own_intra.start()

    rates = [rate_of(z * heads_here + h) for h in range(heads_here)]
    rate_here = jnp.where(core == 0, rates[0], rates[1])
    rate_other = jnp.where(core == 0, rates[1], rates[0])
    for h in range(heads_here):
        fall[h] = jnp.exp(-rates[h] * (place + 1.0))
    chip = CORES * length
    place = lax.broadcasted_iota(jnp.int32, (NX, DH), 0)
    gap = jnp.maximum(x - 1 - place, 0).astype(F32)
    x_coef = jnp.where(place < x, jnp.exp(-rate_here * (chip * gap)), 0.0)
    all_coef = jnp.exp(-rate_here * (chip * (NX - 1 - place).astype(F32)))
    place = lax.broadcasted_iota(jnp.int32, (n_y, DH), 0)
    gap = jnp.maximum(NX * (y - 1 - place) + x, 0).astype(F32)
    y_coef = jnp.where(place < y, jnp.exp(-rate_here * (chip * gap)), 0.0)
    w1 = decay(rate_here, length)

    own_state.wait()
    for d in order:
        z_copy(0, d).wait_recv()
    for h in range(heads_here):
        step_decay = decay(rates[h], part)
        group = state_in[0, h].astype(F32)
        for i in range(1, n_z):
            group = group * step_decay + state_in[i, h].astype(F32)
        gbuf[h] = group

    pair = pltpu.make_async_remote_copy(
        src_ref=gbuf.at[1 - core],
        dst_ref=pair_in,
        send_sem=p_send.at[0],
        recv_sem=p_recv.at[0],
        device_id=partner,
        device_id_type=MESH,
    )
    pair.start()
    pair.wait_recv()
    mine = gbuf[core]
    theirs = pair_in[...]
    first = jnp.where(core == 0, mine, theirs)
    second = jnp.where(core == 0, theirs, mine)
    xbuf[x] = (first * w1 + second).astype(BF16)
    x_copies = []
    for d in range(1, NX):
        copy = pltpu.make_async_remote_copy(
            src_ref=xbuf.at[x],
            dst_ref=xbuf.at[x],
            send_sem=x_send.at[d],
            recv_sem=x_recv.at[d],
            device_id=at_x(d),
            device_id_type=MESH,
        )
        copy.start()
        x_copies.append(copy)
    for copy in x_copies:
        copy.wait_recv()
    in_row = jnp.zeros((DH, DH), F32)
    row_total = jnp.zeros((DH, DH), F32)
    for i in range(NX):
        state = xbuf[i].astype(F32)
        in_row += state * x_coef[i : i + 1]
        row_total += state * all_coef[i : i + 1]
    ybuf[y] = row_total.astype(BF16)

    def y_copy(d):
        return pltpu.make_async_remote_copy(
            src_ref=ybuf.at[y],
            dst_ref=ybuf.at[y],
            send_sem=y_send.at[d],
            recv_sem=y_recv.at[d],
            device_id=at_y(d),
            device_id_type=MESH,
        )

    for d in range(1, n_y):
        y_copy(d).start()
    for d in range(1, n_y):
        y_copy(d).wait_recv()
    incoming = in_row
    for i in range(n_y):
        incoming += ybuf[i].astype(F32) * y_coef[i : i + 1]
    after = incoming * w1 + first
    last_out[...] = jnp.where(core == 0, after, incoming)
    last = pltpu.make_async_remote_copy(
        src_ref=last_out,
        dst_ref=last_in,
        send_sem=p_send.at[1],
        recv_sem=p_recv.at[1],
        device_id=partner,
        device_id_type=MESH,
    )
    last.start()

    loads[3].wait()
    for d in order:
        z_copy(1, d).wait_recv()

    def earlier(h, rate, state):
        cols = pl.ds(pl.multiple_of(h * DH, DH), DH)
        step_decay = decay(rate, part)
        for i in range(n_z):
            rows = slice(i * part, (i + 1) * part)
            high = state.astype(BF16)
            low = (state - high.astype(F32)).astype(BF16)
            query = q_in[rows, cols]
            near[h, rows] = nn(
                jnp.concatenate([query, query], axis=1), jnp.concatenate([high, low], axis=0)
            )
            if i < n_z - 1:
                state = state * step_decay + state_in[i, h].astype(F32)

    earlier(core, rate_here, jnp.where(core == 0, incoming, after))
    last.wait_recv()
    earlier(1 - core, rate_other, last_in[...])

    for d in [0] + order:
        if d:
            z_copy(2, d).wait_recv()
        else:
            own_intra.wait()
        src = lax.rem(z + n_z - d, n_z)
        rows = pl.ds(pl.multiple_of(src * part, part), part)
        for h in range(heads_here):
            cols = slice(h * DH, (h + 1) * DH)
            o = (near[h, rows] + intra_in[rows, cols].astype(F32)) * fall[h]
            scale = lax.rsqrt(jnp.mean(o * o, axis=-1, keepdims=True) + 1e-05)
            out_ref[rows, cols] = (o * scale * gain_ref[:, cols]).astype(BF16)

    for a in range(3):
        for d in order:
            z_copy(a, d).wait_send()
    for copy in x_copies:
        copy.wait_send()
    for d in range(1, n_y):
        y_copy(d).wait_send()
    pair.wait_send()
    last.wait_send()


def body(queries, keys, values, decay_exp, norm_gain):
    _, part, width = queries.shape
    n_z = lax.axis_size("head")
    n_seq = lax.axis_size("seq")
    n_y = n_seq // (NX * CORES)
    wide = width // n_z
    heads_here = wide // DH
    length = part * n_z
    total = length * n_seq
    square = (DH, DH)
    out = pl.pallas_call(
        functools.partial(kernel, n_z, n_y, total),
        out_shape=jax.ShapeDtypeStruct((length, wide), BF16),
        in_specs=[pl.BlockSpec(memory_space=pltpu.HBM)] * 3
        + [pl.BlockSpec(memory_space=pltpu.SMEM), pl.BlockSpec(memory_space=pltpu.VMEM)],
        out_specs=pl.BlockSpec(memory_space=pltpu.VMEM),
        scratch_shapes=[
            pltpu.VMEM((part, width), BF16),
            pltpu.VMEM((part, width), BF16),
            pltpu.VMEM((part, width), BF16),
            pltpu.VMEM((n_z, heads_here) + square, BF16),
            pltpu.VMEM((n_z, heads_here) + square, BF16),
            pltpu.VMEM((n_z, part, wide), BF16),
            pltpu.VMEM((length, wide), BF16),
            pltpu.VMEM((length, wide), BF16),
            pltpu.VMEM((heads_here, length, DH), F32),
            pltpu.VMEM((heads_here, part, DH), F32),
            pltpu.VMEM((heads_here,) + square, F32),
            pltpu.VMEM(square, F32),
            pltpu.VMEM((NX,) + square, BF16),
            pltpu.VMEM((n_y,) + square, BF16),
            pltpu.VMEM(square, F32),
            pltpu.VMEM(square, F32),
            pltpu.SemaphoreType.DMA((6,)),
            pltpu.SemaphoreType.DMA((3, n_z)),
            pltpu.SemaphoreType.DMA((3, n_z)),
            pltpu.SemaphoreType.DMA((NX,)),
            pltpu.SemaphoreType.DMA((NX,)),
            pltpu.SemaphoreType.DMA((n_y,)),
            pltpu.SemaphoreType.DMA((n_y,)),
            pltpu.SemaphoreType.DMA((2,)),
            pltpu.SemaphoreType.DMA((2,)),
        ],
        compiler_params=pltpu.CompilerParams(collective_id=0, has_side_effects=True),
    )(
        queries.reshape(part, width),
        keys.reshape(part, width),
        values.reshape(part, width),
        decay_exp,
        norm_gain.reshape(1, wide),
    )
    return out.reshape(1, length, wide)


def solution(mesh):
    return jax.shard_map(
        body,
        mesh=mesh,
        in_specs=(
            P(None, ("seq", "head"), None),
            P(None, ("seq", "head"), None),
            P(None, ("seq", "head"), None),
            P(),
            P("head"),
        ),
        out_specs=P(None, "seq", "head"),
        check_vma=False,
    )
```

time: 86.1 us -> 66.1 us (0.77)
  Pallas kernels: 84 us -> 64 us
    pallas_call x1, Pallas kernels: 84 us -> 64 us  [body(): pl.pallas_call(functools.partial(kernel, n_z, n_y, total), out_shape=jax....]
where the time goes in v2:
time: 66.1 us; the launch traced here: 65.9 us
  Pallas kernels  64 us (97%)
  local copies, waits for them, and re-layouts  1.97 us (3%)
    pallas_call x1, Pallas kernels, body(): pl.pallas_call(functools.partial(kernel, n_z, n_y, total), out_shape=jax....  64 us
    unnamed x1, local copies, waits for them, and re-layouts  1.97 us

profile of v2, /device:TPU:1, one launch (start us, length us, event | category | flops | bytes accessed | tf_op | source)
XLA Modules:
  0.0 65.9 jit_solution(4071454465957166360)
XLA Ops:
  0.0 64.0 %shard_map.55 = bf16[1280,256]{1,0:T(8,128)(2,1)} custom-call(bf16[160,2048]{1,0:T(8,128)(2,1)} %bitcast.6, bf16[160,2048]{1,0:T(8,128)(2,1)} %bitcast.7, bf16[160,2048]{1,0:T(8,128)(2,1)} %bitcast.8, s32[16]{0:T(128)} %dec_ref.1, f32[1,256]{1,0:T(1,128)} %bitcast.9), custom_call_target="tpu_custom_call" | custom-call | tf_op jit(solution)/shard_map/pallas_call | solution.py:332
  64.0 2.0 %copy.7 = bf16[1,1280,256]{2,1,0:T(8,128)(2,1)} copy(bf16[1,1280,256]{2,1,0:T(8,128)(2,1)} %bitcast.5) | data formatting | bytes 1310720

commit v3 on v2

--- a/solution.py
+++ b/solution.py
@@ -42,9 +42,11 @@
     q_hbm,
     k_hbm,
     v_hbm,
+    dec_hbm,
+    gain_hbm,
+    out_ref,
     dec_ref,
     gain_ref,
-    out_ref,
     qf,
     kf,
     vf,
@@ -95,16 +97,6 @@
 
     partner = (seq_of(y, x, 1 - core), z)
 
-    own_cols = pl.ds(pl.multiple_of(z * wide, wide), wide)
-    own_rows = pl.ds(pl.multiple_of(z * part, part), part)
-    loads = []
-    for a, (src, dst) in enumerate(
-        ((k_hbm, kf), (v_hbm, vf), (q_hbm, qf), (q_hbm.at[:, own_cols], q_in.at[own_rows]))
-    ):
-        copy = pltpu.make_async_copy(src, dst, local_sem.at[a])
-        copy.start()
-        loads.append(copy)
-
     barrier = pltpu.get_barrier_semaphore()
     for d in range(1, n_z):
         pl.semaphore_signal(barrier, inc=1, device_id=at_z(d), device_id_type=MESH)
@@ -114,6 +106,23 @@
         pl.semaphore_signal(barrier, inc=1, device_id=at_y(d), device_id_type=MESH)
     pl.semaphore_signal(barrier, inc=1, device_id=partner, device_id_type=MESH)
 
+    own_cols = pl.ds(pl.multiple_of(z * wide, wide), wide)
+    own_rows = pl.ds(pl.multiple_of(z * part, part), part)
+    loads = []
+    for a, (src, dst) in enumerate(
+        (
+            (k_hbm, kf),
+            (v_hbm, vf),
+            (q_hbm, qf),
+            (q_hbm.at[:, own_cols], q_in.at[own_rows]),
+            (dec_hbm, dec_ref),
+            (gain_hbm, gain_ref),
+        )
+    ):
+        copy = pltpu.make_async_copy(src, dst, local_sem.at[a])
+        copy.start()
+        loads.append(copy)
+
     order = sorted(range(1, n_z), key=lambda d: (-min(d, n_z - d), d))
 
     def rate_of(head):
@@ -123,6 +132,7 @@
         return jnp.exp(jnp.full((1, DH), -rate * tokens, F32))
 
     place = lax.broadcasted_iota(jnp.int32, (part, DH), 0).astype(F32)
+    loads[4].wait()
     loads[0].wait()
     loads[1].wait()
     for d in order + [0]:
@@ -160,7 +170,7 @@
     for a in (0, 1):
         for d in order:
             z_copy(a, d).start()
-    own_state = pltpu.make_async_copy(state_out.at[z], state_in.at[z], local_sem.at[4])
+    own_state = pltpu.make_async_copy(state_out.at[z], state_in.at[z], local_sem.at[6])
     own_state.start()
 
     loads[2].wait()
@@ -179,7 +189,7 @@
             intra_out[to, :, h * DH : (h + 1) * DH] = nn(probs, vf[:, cols]).astype(BF16)
         if d:
             z_copy(2, d).start()
-    own_intra = pltpu.make_async_copy(intra_out.at[z], intra_in.at[own_rows], local_sem.at[5])
+    own_intra = pltpu.make_async_copy(intra_out.at[z], intra_in.at[own_rows], local_sem.at[7])
     own_intra.start()
 
     rates = [rate_of(z * heads_here + h) for h in range(heads_here)]
@@ -274,6 +284,7 @@
     last.start()
 
     loads[3].wait()
+    loads[5].wait()
     for d in order:
         z_copy(1, d).wait_recv()
 
@@ -329,13 +340,15 @@
     length = part * n_z
     total = length * n_seq
     square = (DH, DH)
+    heads = decay_exp.shape[0]
     out = pl.pallas_call(
         functools.partial(kernel, n_z, n_y, total),
-        out_shape=jax.ShapeDtypeStruct((length, wide), BF16),
-        in_specs=[pl.BlockSpec(memory_space=pltpu.HBM)] * 3
-        + [pl.BlockSpec(memory_space=pltpu.SMEM), pl.BlockSpec(memory_space=pltpu.VMEM)],
+        out_shape=pltpu.VMEM((length, wide), BF16),
+        in_specs=[pl.BlockSpec(memory_space=pltpu.HBM)] * 5,
         out_specs=pl.BlockSpec(memory_space=pltpu.VMEM),
         scratch_shapes=[
+            pltpu.SMEM((heads,), jnp.int32),
+            pltpu.VMEM((1, wide), F32),
             pltpu.VMEM((part, width), BF16),
             pltpu.VMEM((part, width), BF16),
             pltpu.VMEM((part, width), BF16),
@@ -352,7 +365,7 @@
             pltpu.VMEM((n_y,) + square, BF16),
             pltpu.VMEM(square, F32),
             pltpu.VMEM(square, F32),
-            pltpu.SemaphoreType.DMA((6,)),
+            pltpu.SemaphoreType.DMA((8,)),
             pltpu.SemaphoreType.DMA((3, n_z)),
             pltpu.SemaphoreType.DMA((3, n_z)),
             pltpu.SemaphoreType.DMA((NX,)),

time: 66.1 us -> 63.4 us (0.959)
  Pallas kernels: 64 us -> 62.4 us
  local copies, waits for them, and re-layouts: 1.97 us -> 0.84 us
    pallas_call x1, Pallas kernels: 64 us -> 62.4 us  [body(): pl.pallas_call(functools.partial(kernel, n_z, n_y, total), out_shape=pltp...]
    unnamed x1, local copies, waits for them, and re-layouts: 1.97 us -> 0.84 us
where the time goes in v3:
time: 63.4 us; the launch traced here: 63.3 us
  Pallas kernels  62.4 us (98%)
  local copies, waits for them, and re-layouts  0.84 us (1%)
    pallas_call x1, Pallas kernels, body(): pl.pallas_call(functools.partial(kernel, n_z, n_y, total), out_shape=pltp...  62.4 us

profile of v3, /device:TPU:1, one launch (start us, length us, event | category | flops | bytes accessed | tf_op | source)
XLA Modules:
  0.0 63.3 jit_solution(13646805790185036776)
XLA Ops:
  0.0 62.4 %shard_map.55 = bf16[1280,256]{1,0:T(8,128)(2,1)S(1)} custom-call(bf16[160,2048]{1,0:T(8,128)(2,1)} %bitcast.6, bf16[160,2048]{1,0:T(8,128)(2,1)} %bitcast.7, bf16[160,2048]{1,0:T(8,128)(2,1)} %bitcast.8, s32[16]{0:T(128)} %dec_hbm.1, f32[1,256]{1,0:T(1,128)} %bitcast.9), custom_call_target="tpu_custom_call" | custom-call | tf_op jit(solution)/shard_map/pallas_call | solution.py:344
  62.5 0.8 %copy.7 = bf16[1,1280,256]{2,1,0:T(8,128)(2,1)} copy(bf16[1,1280,256]{2,1,0:T(8,128)(2,1)S(1)} %bitcast.5) | data formatting | bytes 1310720

commit v4 on v3

--- a/solution.py
+++ b/solution.py
@@ -123,7 +123,8 @@
         copy.start()
         loads.append(copy)
 
-    order = sorted(range(1, n_z), key=lambda d: (-min(d, n_z - d), d))
+    order = sorted(range(1, n_z), key=lambda d: (min(d, n_z - d), d))
+    state_order = sorted(range(1, n_z), key=lambda d: (-min(d, n_z - d), d))
 
     def rate_of(head):
         return power_of_two(dec_ref[head]) / jnp.float32(2.0 * total)
@@ -167,9 +168,10 @@
             device_id_type=MESH,
         )
 
-    for a in (0, 1):
-        for d in order:
-            z_copy(a, d).start()
+    for d in state_order:
+        z_copy(0, d).start()
+    for d in order:
+        z_copy(1, d).start()
     own_state = pltpu.make_async_copy(state_out.at[z], state_in.at[z], local_sem.at[6])
     own_state.start()
 

time: 63.4 us -> 61.1 us (0.964)
  Pallas kernels: 62.4 us -> 60.1 us
    pallas_call x1, Pallas kernels: 62.4 us -> 60.1 us  [body(): pl.pallas_call(functools.partial(kernel, n_z, n_y, total), out_shape=pltp...]
where the time goes in v4:
time: 61.1 us; the launch traced here: 61 us
  Pallas kernels  60.1 us (98%)
  local copies, waits for them, and re-layouts  0.84 us (1%)
    pallas_call x1, Pallas kernels, body(): pl.pallas_call(functools.partial(kernel, n_z, n_y, total), out_shape=pltp...  60.1 us

profile of v4, /device:TPU:1, one launch (start us, length us, event | category | flops | bytes accessed | tf_op | source)
XLA Modules:
  0.0 61.0 jit_solution(2962238947759639523)
XLA Ops:
  0.0 60.1 %shard_map.55 = bf16[1280,256]{1,0:T(8,128)(2,1)S(1)} custom-call(bf16[160,2048]{1,0:T(8,128)(2,1)} %bitcast.6, bf16[160,2048]{1,0:T(8,128)(2,1)} %bitcast.7, bf16[160,2048]{1,0:T(8,128)(2,1)} %bitcast.8, s32[16]{0:T(128)} %dec_hbm.1, f32[1,256]{1,0:T(1,128)} %bitcast.9), custom_call_target="tpu_custom_call" | custom-call | tf_op jit(solution)/shard_map/pallas_call | solution.py:346
  60.1 0.8 %copy.7 = bf16[1,1280,256]{2,1,0:T(8,128)(2,1)} copy(bf16[1,1280,256]{2,1,0:T(8,128)(2,1)S(1)} %bitcast.5) | data formatting | bytes 1310720
